TPU v7x, 32 devices: a whole 2x2x4 slice. The times are simulated.
32 devices in a mesh: groups: 2 (over x), expert: 16 (over z, y, core).
Axes of the slice: x: 2, y: 2, z: 4, core: 2. Of those that a mesh axis runs over, the one named last changes fastest.
Arguments:
- residual: bfloat16 [512, 2880], P(('groups', 'expert')), parts along dimension 0, may hold values from -6 to 6
- norm_gain: float32 [2880], replicated, may hold values from 0.1 to 1.9
- expert_ids: int32 [512, 4], P(('groups', 'expert')), parts along dimension 0, may hold values from 0 to 7, all different within a row; in each aligned block of 16 rows (0 to 15, 16 to 31, ...) at most 16 rows name the same one
- expert_weights: float32 [512, 4], P(('groups', 'expert')), parts along dimension 0, may hold values from 0.2 to 1
- gate_proj: bfloat16 [16, 2880, 720], P('expert'), may hold values from -0.109375 to 0.109375
- up_proj: bfloat16 [16, 2880, 720], P('expert'), may hold values from -0.109375 to 0.109375
- down_proj: bfloat16 [16, 720, 2880], P('expert'), may hold values from -0.15625 to 0.15625
Outputs:
- mixed: bfloat16 [512, 2880], P(('groups', 'expert')), parts along dimension 0
There are 2 independent parts, one for each index of `groups`. A program takes and returns all parts, laid end to end along the dimension named above; an argument that names none is the same for every part. Nothing has to cross between parts.
Inputs may be any that keep to these rules, and one draw needn't show every extreme that they name: `expert_ids`: in each aligned block of 16 rows (the rows of one device) no expert is named by more than 16 entries.
All inputs are finite; a program needn't handle non-finite values.
Results may differ from a plain program's by a relative error of at most 0.0063.
Values may be sent and summed in bfloat16 or wider, within the bound.
A program may use at most 64 MiB of HBM per device.

v0:
```python
import functools

import jax
import jax.numpy as jnp
from jax import lax
from jax.experimental import pallas as pl
from jax.experimental.pallas import tpu as pltpu
from jax.sharding import PartitionSpec as P

BF16 = jnp.bfloat16
F32 = jnp.float32
LANES = 128


def partner(value, axis, bit):
    mask = 2**bit
    pairs = [(source, source ^ mask) for source in range(lax.axis_size(axis))]
    return lax.ppermute(value, axis, pairs)


def expert_half(block, gate_w, up_w, down_w):
    flat = block.reshape(-1, block.shape[-1])
    gate = jnp.dot(flat, gate_w, preferred_element_type=jnp.float32)
    upper = jnp.dot(flat, up_w, preferred_element_type=jnp.float32)
    act = (gate * jax.nn.sigmoid(1.702 * gate) * (upper + 1.0)).astype(jnp.bfloat16)
    out = jnp.dot(act, down_w, preferred_element_type=jnp.float32).astype(jnp.bfloat16)
    return out.reshape(block.shape[:-1] + (down_w.shape[1],))


def slotted(residual, norm_gain, expert_ids, expert_weights, gate_proj, up_proj, down_proj):
    rows, model = residual.shape
    chosen = expert_ids.shape[1]
    devices = lax.axis_size("expert")
    experts = devices // 2
    capacity = 2 * rows * chosen // experts
    half_cap = capacity // 2
    gate_w, up_w, down_w = (gate_proj[0], up_proj[0], down_proj[0])
    x = residual.astype(jnp.float32)
    scale = lax.rsqrt(jnp.mean(x * x, axis=-1, keepdims=True) + 1e-05)
    normed = (x * scale * norm_gain).astype(jnp.bfloat16)
    flat_ids = expert_ids.reshape(rows * chosen)
    onehot = (
        flat_ids[:, None] == lax.broadcasted_iota(jnp.int32, (rows * chosen, experts), 1)
    ).astype(jnp.int32)
    slot = jnp.sum(onehot * jnp.cumsum(onehot, axis=0), axis=1) - 1
    position = flat_ids * capacity + slot
    pick = (
        position[:, None] == lax.broadcasted_iota(jnp.int32, (rows * chosen, experts * capacity), 1)
    ).astype(jnp.float32)
    place_rows = jnp.sum(pick.reshape(rows, chosen, experts * capacity), axis=1)
    send = lax.dot_general(
        place_rows.astype(jnp.bfloat16),
        normed,
        (((0,), (0,)), ((), ())),
        preferred_element_type=jnp.float32,
    )
    send = send.astype(jnp.bfloat16).reshape(experts, capacity, model)
    outgoing = send.reshape(experts, 2, half_cap, model).reshape(devices, half_cap, model)
    arrived = lax.all_to_all(outgoing, "expert", split_axis=0, concat_axis=0, tiled=True)
    other = partner(arrived, "expert", 0)
    both = expert_half(jnp.stack((arrived, other)), gate_w, up_w, down_w)
    returned = partner(both[1], "expert", 0)
    finished = (both[0].astype(jnp.float32) + returned.astype(jnp.float32)).astype(jnp.bfloat16)
    back = lax.all_to_all(finished, "expert", split_axis=0, concat_axis=0, tiled=True)
    results = back.reshape(experts, capacity, model)
    weighted = jnp.sum(
        (pick * expert_weights.reshape(rows * chosen)[:, None]).reshape(
            rows, chosen, experts * capacity
        ),
        axis=1,
    )
    combined = jnp.dot(
        weighted,
        results.reshape(experts * capacity, model).astype(jnp.float32),
        precision=lax.Precision.HIGHEST,
    )
    return (x + combined).astype(jnp.bfloat16)


def cuts(total, shares):
    unit = 2 * LANES
    whole = sum(shares)
    ends = [round(total * sum(shares[: n + 1]) / whole / unit) * unit for n in range(len(shares))]
    ends = sorted(set(min(max(e, unit), total) for e in ends[:-1]) | {total})
    starts = [0] + ends[:-1]
    return [(s, e - s) for s, e in zip(starts, ends) if e > s]


def kernel(
    line, experts, in_cuts, out_cuts,
    res_ref, gain_ref, ids_ref, wts_ref, gate_hbm, up_hbm, down_hbm, out_ref,
    gate_v, up_v, down_v, xg, gacc, uacc, part, core_r, y_s, y_r, z_s, z_r,
    w_sem, d_sem, agl_s, agr_s, agz_r, agy_s, agy_r, agc_s, agc_r,
    rc_s, rc_r, ry_s, ry_r, rz_s, rz_r,
):
    rows, model = res_ref.shape
    extra = xg.shape[1] - model
    halves, short = 1, rows
    tokens = 4 * line * short
    half, quarter = tokens // 2, tokens // 4
    me = lax.axis_index("expert")
    core = lax.rem(me, 2)
    y = lax.rem(me // 2, 2)
    z = me // 4

    def device(z_, y_, c_):
        return (z_ * 2 + y_) * 2 + c_

    def row(h, z_, y_, c_):
        return pl.multiple_of(((c_ * 2 + y_) * line + z_) * short + h * tokens, short)

    def remote(src, dst, send, recv, target):
        return pltpu.make_async_remote_copy(
            src_ref=src, dst_ref=dst, send_sem=send, recv_sem=recv,
            device_id={"expert": target}, device_id_type=pl.DeviceIdType.MESH,
        )

    if line == 4:
        inner = lax.rem((z + 1) // 2, 2)
        beside = z + 1 - 2 * lax.rem(z, 2)
        skip, mirror = lax.rem(z + 2, 4), 3 - z
        others = [
            beside,
            inner * mirror + (1 - inner) * skip,
            inner * skip + (1 - inner) * mirror,
        ]
    else:
        others = [lax.rem(z + o, line) for o in range(1, line)]
    y_dev = device(z, 1 - y, core)
    c_dev = device(z, y, 1 - core)

    loads = []
    for k, (at, wide) in enumerate(in_cuts):
        pair = []
        for n, (hbm, vmem) in enumerate(((gate_hbm, gate_v), (up_hbm, up_v))):
            copy = pltpu.make_async_copy(
                hbm.at[0, :, pl.ds(at, wide)], vmem.at[:, pl.ds(at, wide)], w_sem.at[k, n]
            )
            copy.start()
            pair.append(copy)
        loads.append(pair)
    down_load = pltpu.make_async_copy(down_hbm.at[0], down_v, d_sem)
    down_load.start()

    barrier = pltpu.get_barrier_semaphore()
    last = line - 1
    has_left = (z + last) // line
    has_right = (2 * last - z) // line

    def greet(peer):
        pl.semaphore_signal(
            barrier, inc=1, device_id={"expert": peer}, device_id_type=pl.DeviceIdType.MESH
        )

    greet(y_dev)
    greet(c_dev)
    pl.when(z > 0)(lambda: greet(device(z - 1, y, core)))
    pl.when(z < last)(lambda: greet(device(z + 1, y, core)))

    x = res_ref[...].astype(F32)
    scale = lax.rsqrt(jnp.mean(x * x, axis=-1, keepdims=True) + 1e-05)
    normed = (x * scale * gain_ref[...]).astype(BF16)
    named = lax.broadcasted_iota(jnp.int32, (extra, rows), 0)
    high = jnp.zeros((extra, rows), F32)
    low = jnp.zeros((extra, rows), F32)
    for k in range(ids_ref.shape[0]):
        ids = ids_ref[k : k + 1, :]
        high = high + jnp.where(ids == named, wts_ref[k : k + 1, :], 0.0)
        low = low + jnp.where(ids + experts == named, wts_ref[k : k + 1, :], 0.0)
    rest = low - low.astype(BF16).astype(F32)
    shares = jnp.transpose(high + rest).astype(BF16)
    for h in range(halves):
        mine = pl.ds(row(h, z, y, core), short)
        xg[mine, 0:model] = normed[h * short : (h + 1) * short]
        xg[mine, model : model + extra] = shares[h * short : (h + 1) * short]

    pl.semaphore_wait(barrier, 2 + has_left + has_right)

    sent = []

    def go(copy):
        copy.start()
        sent.append(copy)

    chunks = len(in_cuts)

    def block(k, z_, y_, c_, count):
        at, wide = in_cuts[k]
        if k == chunks - 1:
            wide = wide + extra
        return xg.at[pl.ds(row(0, z_, y_, c_), count * short), pl.ds(at, wide)]

    def pass_left(k, z_):
        at = block(k, z_, y, core, 1)
        return remote(at, at, agl_s.at[k, z_], agz_r.at[k, z_], device(z - 1, y, core))

    def pass_right(k, z_):
        at = block(k, z_, y, core, 1)
        return remote(at, at, agr_s.at[k, z_], agz_r.at[k, z_], device(z + 1, y, core))

    def pass_y(k, z_):
        at = block(k, z_, y, core, 1)
        return remote(at, at, agy_s.at[k, z_], agy_r.at[k, z_], y_dev)

    def from_right(k, d):
        pass_left(k, z + d).wait_recv()
        pass_y(k, z + d).start()
        pl.when(z > 0)(lambda: pass_left(k, z + d).start())

    def from_left(k, d):
        pass_right(k, z - d).wait_recv()
        pass_y(k, z - d).start()
        pl.when(z < last)(lambda: pass_right(k, z - d).start())

    for k in range(chunks):
        pass_y(k, z).start()
        pl.when(z > 0)(lambda: pass_left(k, z).start())
        pl.when(z < last)(lambda: pass_right(k, z).start())

    def line_step(d, k):
        pl.when(z + d <= last)(lambda: from_right(k, d))
        pl.when(z - d >= 0)(lambda: from_left(k, d))

    def core_group(k, n):
        group = block(k, 0, y if n == 0 else 1 - y, core, line)
        go(remote(group, group, agc_s.at[k, n], agc_r.at[k, n], c_dev))

    def relay_y(k):
        for there in range(line):
            got = block(k, there, 1 - y, core, 1)
            remote(got, got, agy_s.at[k, there], agy_r.at[k, there], y_dev).wait_recv()
        core_group(k, 1)

    def arrive(k):
        for n, y_ in enumerate((y, 1 - y)):
            group = block(k, 0, y_, 1 - core, line)
            remote(group, group, agc_s.at[k, n], agc_r.at[k, n], c_dev).wait_recv()

    def drain_gather():
        for k in range(chunks):
            for z_ in range(line):
                pass_y(k, z_).wait_send()
                pl.when(jnp.logical_and(z > 0, z <= z_))(
                    lambda: pass_left(k, z_).wait_send()
                )
                pl.when(jnp.logical_and(z < last, z >= z_))(
                    lambda: pass_right(k, z_).wait_send()
                )

    expert = me // 2

    def multiply(k):
        at, wide = in_cuts[k]
        for n, (vmem, acc) in enumerate(((gate_v, gacc), (up_v, uacc))):
            loads[k][n].wait()
            product = lax.dot_general(
                xg[:, at : at + wide], vmem[:, at : at + wide], (((1,), (1,)), ((), ())),
                preferred_element_type=F32,
            )
            if k == 0:
                acc[...] = product
            else:
                acc[...] += product

    def hidden():
        gate = gacc[...]
        act = (gate * jax.nn.sigmoid(1.702 * gate) * (uacc[...] + 1.0)).astype(BF16)
        lanes = lax.broadcasted_iota(jnp.int32, (tokens, extra), 1)
        ours = jnp.logical_or(lanes == expert, lanes == expert + experts)
        weight = jnp.sum(
            jnp.where(ours, xg[:, model : model + extra].astype(F32), 0.0),
            axis=1, keepdims=True,
        )
        return act, weight

    my_half = core * half
    its_half = (1 - core) * half
    my_y = y * quarter
    its_y = (1 - y) * quarter

    def at_row(value, unit):
        return pl.multiple_of(value, unit)

    def core_copy(h, j):
        at, wide = out_cuts[j]
        cols = pl.ds(at, wide)
        return remote(
            part.at[pl.ds(at_row(its_half + h * tokens, half), half), cols],
            core_r.at[pl.ds(h * half, half), cols],
            rc_s.at[h, j], rc_r.at[h, j], c_dev,
        )

    def y_copy(h, j):
        at, wide = out_cuts[j]
        spot = (pl.ds(h * quarter, quarter), pl.ds(at, wide))
        return remote(y_s.at[spot], y_r.at[spot], ry_s.at[h, j], ry_r.at[h, j], y_dev)

    def z_copy(h, j, there):
        at, wide = out_cuts[j]
        cols = pl.ds(at, wide)
        return remote(
            z_s.at[pl.ds(at_row(h * quarter + there * short, short), short), cols],
            z_r.at[pl.ds(at_row(h * quarter + z * short, short), short), cols],
            rz_s.at[h, j, there], rz_r.at[h, j, z], device(there, y, core),
        )

    def z_arrival(h, j, there):
        at, wide = out_cuts[j]
        spot = (pl.ds(at_row(h * quarter + there * short, short), short), pl.ds(at, wide))
        return remote(
            z_r.at[spot], z_r.at[spot], rz_s.at[h, j, there], rz_r.at[h, j, there], c_dev
        )

    def first(h, j, act, weight):
        at, wide = out_cuts[j]
        product = jnp.dot(act, down_v[:, at : at + wide], preferred_element_type=F32)
        part[h * tokens : (h + 1) * tokens, at : at + wide] = (product * weight).astype(BF16)
        go(core_copy(h, j))

    def pair_sum(h, j, which):
        at, wide = out_cuts[j]
        theirs = core_r[pl.ds(at_row(h * half + which, quarter), quarter), at : at + wide]
        here = part[
            pl.ds(at_row(h * tokens + my_half + which, quarter), quarter), at : at + wide
        ]
        return theirs.astype(F32) + here.astype(F32)

    def second(h, j):
        at, wide = out_cuts[j]
        core_copy(h, j).wait_recv()
        y_s[h * quarter : (h + 1) * quarter, at : at + wide] = pair_sum(h, j, its_y).astype(BF16)
        go(y_copy(h, j))

    def third(h, j):
        at, wide = out_cuts[j]
        total = pair_sum(h, j, my_y)
        y_copy(h, j).wait_recv()
        span = slice(h * quarter, (h + 1) * quarter)
        total = total + y_r[span, at : at + wide].astype(F32)
        z_s[span, at : at + wide] = total.astype(BF16)
        for there in others[::-1]:
            go(z_copy(h, j, there))

    def fourth(h, j):
        at, wide = out_cuts[j]
        own = pl.ds(at_row(h * quarter + z * short, short), short)
        total = z_s[own, at : at + wide].astype(F32)
        for there in others:
            z_arrival(h, j, there).wait_recv()
            spot = pl.ds(at_row(h * quarter + there * short, short), short)
            total = total + z_r[spot, at : at + wide].astype(F32)
        span = slice(h * short, (h + 1) * short)
        out_ref[span, at : at + wide] = (
            res_ref[span, at : at + wide].astype(F32) + total
        ).astype(BF16)

    pieces = range(len(out_cuts))
    for d in range(1, line):
        for k in range(chunks):
            line_step(d, k)
            if d == last:
                core_group(k, 0)
    for k in range(chunks):
        relay_y(k)
    for k in range(chunks):
        arrive(k)
        multiply(k)
    act, weight = hidden()
    down_load.wait()
    lags = (0, 1, 3)
    for step in range(len(out_cuts) + lags[-1]):
        for lag, stage in zip(lags, (first, second, third)):
            if 0 <= step - lag < len(out_cuts):
                if stage is first:
                    first(0, step, act, weight)
                else:
                    stage(0, step - lag)
    for h in range(halves):
        for j in pieces:
            fourth(h, j)
    drain_gather()
    for copy in sent:
        copy.wait_send()


def fused(residual, norm_gain, expert_ids, expert_weights, gate_proj, up_proj, down_proj):
    rows, model = residual.shape
    hidden = gate_proj.shape[2]
    devices = lax.axis_size("expert")
    experts = devices // 2
    line = devices // 4
    halves = 1
    in_cuts = cuts(model, (4, 4, 3))
    ins = len(in_cuts)
    tokens = rows * devices
    width = -(-(model + 2 * experts) // LANES) * LANES
    out_cuts = cuts(model, (2, 3, 3, 2, 1))
    outs = len(out_cuts)
    vmem = pl.BlockSpec(memory_space=pltpu.VMEM)
    hbm = pl.BlockSpec(memory_space=pl.ANY)
    dma = pltpu.SemaphoreType.DMA
    return pl.pallas_call(
        functools.partial(kernel, line, experts, in_cuts, out_cuts),
        out_shape=jax.ShapeDtypeStruct((rows, model), BF16),
        in_specs=[vmem] * 4 + [hbm] * 3,
        out_specs=vmem,
        scratch_shapes=[
            pltpu.VMEM((hidden, model), BF16),
            pltpu.VMEM((hidden, model), BF16),
            pltpu.VMEM((hidden, model), BF16),
            pltpu.VMEM((tokens, width), BF16),
            pltpu.VMEM((tokens, hidden), F32),
            pltpu.VMEM((tokens, hidden), F32),
            pltpu.VMEM((tokens, model), BF16),
            pltpu.VMEM((tokens // 2, model), BF16),
            pltpu.VMEM((tokens // 4, model), BF16),
            pltpu.VMEM((tokens // 4, model), BF16),
            pltpu.VMEM((tokens // 4, model), BF16),
            pltpu.VMEM((tokens // 4, model), BF16),
            dma((ins, 2)),
            dma,
            dma((ins, line)),
            dma((ins, line)),
            dma((ins, line)),
            dma((ins, line)),
            dma((ins, line)),
            dma((ins, 2)),
            dma((ins, 2)),
            dma((halves, outs)),
            dma((halves, outs)),
            dma((halves, outs)),
            dma((halves, outs)),
            dma((halves, outs, line)),
            dma((halves, outs, line)),
        ],
        compiler_params=pltpu.CompilerParams(
            collective_id=0, has_side_effects=True, vmem_limit_bytes=60 * 1024 * 1024
        ),
    )(
        residual, norm_gain, expert_ids.T, expert_weights.T,
        gate_proj.transpose(0, 2, 1), up_proj.transpose(0, 2, 1), down_proj,
    )


def body(residual, norm_gain, expert_ids, expert_weights, gate_proj, up_proj, down_proj):
    rows = residual.shape[0]
    devices = lax.axis_size("expert")
    capacity = 4 * rows * expert_ids.shape[1] // devices
    dense = capacity >= rows and devices % 4 == 0
    form = fused if dense else slotted
    return form(
        residual, norm_gain, expert_ids, expert_weights, gate_proj, up_proj, down_proj
    )


def solution(mesh):
    in_specs = (
        P(("groups", "expert"), None),
        P(),
        P(("groups", "expert"), None),
        P(("groups", "expert"), None),
        P("expert", None, None),
        P("expert", None, None),
        P("expert", None, None),
    )
    out_specs = P(("groups", "expert"), None)
    return jax.shard_map(body, mesh=mesh, in_specs=in_specs, out_specs=out_specs, check_vma=False)
```

profile of v0, /device:TPU:0, one launch (start us, length us, event | category | flops | bytes accessed | tf_op | source)
XLA Modules:
  0.0 40.6 jit_solution(5074138144492457515)
XLA Ops:
  0.0 39.1 %shard_map.73 = bf16[16,2880]{1,0:T(8,128)(2,1)} custom-call(bf16[16,2880]{1,0:T(8,128)(2,1)} %res_ref.1, f32[2880]{0:T(1024)} %gain_ref.1, s32[4,16]{1,0:T(4,128)} %bitcast.6, f32[4,16]{1,0:T(4,128)} %bitcast.7, bf16[1,720,2880]{2,1,0:T(8,128)(2,1)} %bitcast.4, bf16[1,720,2880]{2,1,0:T(8,128)(2,1)} %bitcast.5, bf16[1,720,2880]{2,1,0:T(8,128)(2,1)} %down_hbm.1), custom_call_target="tpu_custom_call" | custom-call | tf_op jit(solution)/shard_map/pallas_call | solution.py:402
  39.1 1.5 %copy.9 = bf16[16,2880]{1,0:T(8,128)(2,1)} copy(bf16[16,2880]{1,0:T(8,128)(2,1)} %shard_map.73) | data formatting | bytes 184320
where the time goes:
time: 40.8 us; the launch traced here: 40.6 us
  Pallas kernels  39.1 us (96%)
  local copies, waits for them, and re-layouts  1.54 us (4%)
    pallas_call x1, Pallas kernels, fused(): pl.pallas_call(functools.partial(kernel, line, experts, in_cuts, out_cuts...  39.1 us
    unnamed x1, local copies, waits for them, and re-layouts  1.54 us

commit v1 on v0

v1 whole, which is shorter than its diff:
```python
import functools

import jax
import jax.numpy as jnp
from jax import lax
from jax.experimental import pallas as pl
from jax.experimental.pallas import tpu as pltpu
from jax.sharding import PartitionSpec as P

BF16 = jnp.bfloat16
F32 = jnp.float32
LANES = 128


def partner(value, axis, bit):
    mask = 2**bit
    pairs = [(source, source ^ mask) for source in range(lax.axis_size(axis))]
    return lax.ppermute(value, axis, pairs)


def expert_half(block, gate_w, up_w, down_w):
    flat = block.reshape(-1, block.shape[-1])
    gate = jnp.dot(flat, gate_w, preferred_element_type=jnp.float32)
    upper = jnp.dot(flat, up_w, preferred_element_type=jnp.float32)
    act = (gate * jax.nn.sigmoid(1.702 * gate) * (upper + 1.0)).astype(jnp.bfloat16)
    out = jnp.dot(act, down_w, preferred_element_type=jnp.float32).astype(jnp.bfloat16)
    return out.reshape(block.shape[:-1] + (down_w.shape[1],))


def slotted(residual, norm_gain, expert_ids, expert_weights, gate_proj, up_proj, down_proj):
    rows, model = residual.shape
    chosen = expert_ids.shape[1]
    devices = lax.axis_size("expert")
    experts = devices // 2
    capacity = 2 * rows * chosen // experts
    half_cap = capacity // 2
    gate_w, up_w, down_w = (gate_proj[0], up_proj[0], down_proj[0])
    x = residual.astype(jnp.float32)
    scale = lax.rsqrt(jnp.mean(x * x, axis=-1, keepdims=True) + 1e-05)
    normed = (x * scale * norm_gain).astype(jnp.bfloat16)
    flat_ids = expert_ids.reshape(rows * chosen)
    onehot = (
        flat_ids[:, None] == lax.broadcasted_iota(jnp.int32, (rows * chosen, experts), 1)
    ).astype(jnp.int32)
    slot = jnp.sum(onehot * jnp.cumsum(onehot, axis=0), axis=1) - 1
    position = flat_ids * capacity + slot
    pick = (
        position[:, None] == lax.broadcasted_iota(jnp.int32, (rows * chosen, experts * capacity), 1)
    ).astype(jnp.float32)
    place_rows = jnp.sum(pick.reshape(rows, chosen, experts * capacity), axis=1)
    send = lax.dot_general(
        place_rows.astype(jnp.bfloat16),
        normed,
        (((0,), (0,)), ((), ())),
        preferred_element_type=jnp.float32,
    )
    send = send.astype(jnp.bfloat16).reshape(experts, capacity, model)
    outgoing = send.reshape(experts, 2, half_cap, model).reshape(devices, half_cap, model)
    arrived = lax.all_to_all(outgoing, "expert", split_axis=0, concat_axis=0, tiled=True)
    other = partner(arrived, "expert", 0)
    both = expert_half(jnp.stack((arrived, other)), gate_w, up_w, down_w)
    returned = partner(both[1], "expert", 0)
    finished = (both[0].astype(jnp.float32) + returned.astype(jnp.float32)).astype(jnp.bfloat16)
    back = lax.all_to_all(finished, "expert", split_axis=0, concat_axis=0, tiled=True)
    results = back.reshape(experts, capacity, model)
    weighted = jnp.sum(
        (pick * expert_weights.reshape(rows * chosen)[:, None]).reshape(
            rows, chosen, experts * capacity
        ),
        axis=1,
    )
    combined = jnp.dot(
        weighted,
        results.reshape(experts * capacity, model).astype(jnp.float32),
        precision=lax.Precision.HIGHEST,
    )
    return (x + combined).astype(jnp.bfloat16)


def cuts(total, shares):
    unit = 2 * LANES
    whole = sum(shares)
    ends = [round(total * sum(shares[: n + 1]) / whole / unit) * unit for n in range(len(shares))]
    ends = sorted(set(min(max(e, unit), total) for e in ends[:-1]) | {total})
    starts = [0] + ends[:-1]
    return [(s, e - s) for s, e in zip(starts, ends) if e > s]


def kernel(
    experts, in_cuts, out_cuts,
    res_ref, gain_ref, ids_ref, wts_ref, gate_hbm, up_hbm, down_hbm, out_ref,
    gate_v, up_v, down_v, xg, gacc, uacc, act_v, part, core_r, y_s, y_r, z_s, z_r,
    w_sem, d_sem, agl_s, agr_s, agz_r, agy_s, agy_r, agc_s, agc_r,
    rc_s, rc_r, ry_s, ry_r, rz_s, rz_r,
):
    line = 4
    last = line - 1
    rows, model = res_ref.shape
    extra = xg.shape[1] - model
    tokens = 4 * line * rows
    half, pair = tokens // 2, tokens // 4
    me = lax.axis_index("expert")
    core = lax.rem(me, 2)
    y = lax.rem(me // 2, 2)
    z = me // 4
    side, low = z // 2, lax.rem(z, 2)
    near, far = z + 1 - 2 * low, lax.rem(z + 2, line)

    def device(z_, y_, c_):
        return (z_ * 2 + y_) * 2 + c_

    def row(z_, y_, c_):
        at = (((z_ // 2 * 2 + c_) * 2 + lax.rem(z_, 2)) * 2 + y_) * rows
        return pl.multiple_of(at, rows)

    def remote(src, dst, send, recv, target):
        return pltpu.make_async_remote_copy(
            src_ref=src, dst_ref=dst, send_sem=send, recv_sem=recv,
            device_id={"expert": target}, device_id_type=pl.DeviceIdType.MESH,
        )

    y_dev = device(z, 1 - y, core)
    c_dev = device(z, y, 1 - core)
    n_dev = device(near, y, core)
    f_dev = device(far, y, core)

    barrier = pltpu.get_barrier_semaphore()
    inner = jnp.logical_and(z > 0, z < last)

    def greet(peer):
        pl.semaphore_signal(
            barrier, inc=1, device_id={"expert": peer}, device_id_type=pl.DeviceIdType.MESH
        )

    greet(y_dev)
    greet(c_dev)
    greet(n_dev)
    greet(f_dev)
    pl.when(inner)(lambda: greet(device(last - z, y, core)))

    loads = []
    for n, (hbm, vmem) in enumerate(((gate_hbm, gate_v), (up_hbm, up_v))):
        loads.append(pltpu.make_async_copy(hbm.at[0], vmem, w_sem.at[n]))
    loads.append(pltpu.make_async_copy(down_hbm.at[0], down_v, d_sem))
    for copy in loads:
        copy.start()

    x = res_ref[...].astype(F32)
    scale = lax.rsqrt(jnp.mean(x * x, axis=-1, keepdims=True) + 1e-05)
    normed = (x * scale * gain_ref[...]).astype(BF16)
    named = lax.broadcasted_iota(jnp.int32, (extra, rows), 0)
    high = jnp.zeros((extra, rows), F32)
    under = jnp.zeros((extra, rows), F32)
    for k in range(ids_ref.shape[0]):
        ids = ids_ref[k : k + 1, :]
        high = high + jnp.where(ids == named, wts_ref[k : k + 1, :], 0.0)
        under = under + jnp.where(ids + experts == named, wts_ref[k : k + 1, :], 0.0)
    rest = under - under.astype(BF16).astype(F32)
    shares = jnp.transpose(high + rest).astype(BF16)
    mine = pl.ds(row(z, y, core), rows)
    xg[mine, 0:model] = normed
    xg[mine, model : model + extra] = shares

    pl.semaphore_wait(barrier, 4 + jnp.where(inner, 1, 0))

    chunks = len(in_cuts)

    def columns(k):
        at, wide = in_cuts[k]
        return pl.ds(at, wide + extra if k == chunks - 1 else wide)

    def block(k, z_, y_, c_):
        return xg.at[pl.ds(row(z_, y_, c_), rows), columns(k)]

    def pass_left(k, z_):
        at = block(k, z_, y, core)
        return remote(at, at, agl_s.at[k, z_], agz_r.at[k, z_], device(z - 1, y, core))

    def pass_right(k, z_):
        at = block(k, z_, y, core)
        return remote(at, at, agr_s.at[k, z_], agz_r.at[k, z_], device(z + 1, y, core))

    def pass_y(k, z_):
        at = block(k, z_, y, core)
        return remote(at, at, agy_s.at[k], agy_r.at[k, z_], y_dev)

    def from_y(k, z_):
        at = block(k, z_, 1 - y, core)
        return remote(at, at, agy_s.at[k], agy_r.at[k, z_], y_dev)

    def pass_core(k, z_, y_):
        at = block(k, z_, y_, core)
        remote(at, at, agc_s.at[k], agc_r.at[k], c_dev).start()

    def bulk(k, count):
        return xg.at[pl.ds(0, count * rows), columns(k)]

    def from_right(k, d):
        pass_left(k, z + d).wait_recv()
        pass_y(k, z + d).start()
        pl.when(z > 0)(lambda: pass_left(k, z + d).start())
        pass_core(k, z + d, y)

    def from_left(k, d):
        pass_right(k, z - d).wait_recv()
        pass_y(k, z - d).start()
        pl.when(z < last)(lambda: pass_right(k, z - d).start())
        pass_core(k, z - d, y)

    def line_step(k, d):
        pl.when(z + d <= last)(lambda: from_right(k, d))
        pl.when(z - d >= 0)(lambda: from_left(k, d))

    for k in range(chunks):
        pass_y(k, z).start()
        pl.when(z > 0)(lambda: pass_left(k, z).start())
        pl.when(z < last)(lambda: pass_right(k, z).start())
    for k in range(chunks):
        pass_core(k, z, y)
    for d in range(1, line):
        for k in range(chunks):
            line_step(k, d)
    for k in range(chunks):
        for there in range(line):
            from_y(k, there).wait_recv()
            pass_core(k, there, 1 - y)

    def arrive(k):
        at = bulk(k, 2 * line)
        remote(at, at, agc_s.at[k], agc_r.at[k], c_dev).wait_recv()

    def drain_gather():
        for k in range(chunks):
            at = bulk(k, line)
            remote(at, at, agy_s.at[k], agy_r.at[k, 0], y_dev).wait_send()
            at = bulk(k, 2 * line)
            remote(at, at, agc_s.at[k], agc_r.at[k], c_dev).wait_send()
            for z_ in range(line):
                pl.when(jnp.logical_and(z > 0, z <= z_))(
                    lambda: pass_left(k, z_).wait_send()
                )
                pl.when(jnp.logical_and(z < last, z >= z_))(
                    lambda: pass_right(k, z_).wait_send()
                )

    expert = me // 2
    swap = (((1,), (1,)), ((), ()))

    loads[0].wait()
    loads[1].wait()
    for k in range(chunks - 1):
        arrive(k)
    split = in_cuts[-1][0]
    for vmem, acc in ((gate_v, gacc), (up_v, uacc)):
        acc[...] = lax.dot_general(
            vmem[:, 0:split], xg[:, 0:split], swap, preferred_element_type=F32
        )
    arrive(chunks - 1)
    loads[2].wait()
    gate, upper = (
        acc[...] + lax.dot_general(
            vmem[:, split:model], xg[:, split:model], swap, preferred_element_type=F32
        )
        for vmem, acc in ((gate_v, gacc), (up_v, uacc))
    )
    act_v[...] = (gate * jax.nn.sigmoid(1.702 * gate) * (upper + 1.0)).astype(BF16).T

    bases = (
        pl.multiple_of((1 - side) * half, half),
        pl.multiple_of(side * half, half),
    )
    lanes = lax.broadcasted_iota(jnp.int32, (tokens, extra), 1)
    ours = jnp.logical_or(lanes == expert, lanes == expert + experts)
    weight = jnp.sum(
        jnp.where(ours, xg[:, model : model + extra].astype(F32), 0.0), axis=1, keepdims=True
    )
    outs = range(len(out_cuts))

    def core_copy(h, j):
        at, wide = out_cuts[j]
        cols = pl.ds(at, wide)
        theirs = pl.multiple_of(bases[h] + (1 - core) * pair, pair)
        return remote(
            part.at[pl.ds(theirs, pair), cols],
            core_r.at[pl.ds(h * pair, pair), cols],
            rc_s, rc_r.at[h, j], c_dev,
        )

    def product(j):
        at, wide = out_cuts[j]
        value = jnp.dot(act_v[...], down_v[:, at : at + wide], preferred_element_type=F32)
        part[:, at : at + wide] = (value * weight).astype(BF16)
        core_copy(0, j).start()

    def pair_sum(h, j, low_, y_):
        at, wide = out_cuts[j]
        inside = (low_ * 2 + y_) * rows
        theirs = core_r[pl.ds(pl.multiple_of(h * pair + inside, rows), rows), at : at + wide]
        spot = pl.multiple_of(bases[h] + core * pair + inside, rows)
        here = part[pl.ds(spot, rows), at : at + wide]
        return theirs.astype(F32) + here.astype(F32)

    spots = ((0, 2), (2, 1), (3, 1))
    FAR, NEAR, OWN = range(3)

    def y_copy(g, j):
        at, wide = out_cuts[j]
        first, count = spots[g]
        spot = (pl.ds(first * rows, count * rows), pl.ds(at, wide))
        return remote(y_s.at[spot], y_r.at[spot], ry_s, ry_r.at[g, j], y_dev)

    def slot(i, j):
        at, wide = out_cuts[j]
        return slice(i * rows, (i + 1) * rows), slice(at, at + wide)

    def y_send(g, j):
        if g == FAR:
            core_copy(0, j).wait_recv()
            y_s[slot(0, j)] = pair_sum(0, j, low, 1 - y).astype(BF16)
            y_s[slot(1, j)] = pair_sum(0, j, 1 - low, 1 - y).astype(BF16)
        elif g == NEAR:
            core_copy(1, j).wait_recv()
            y_s[slot(2, j)] = pair_sum(1, j, 1 - low, 1 - y).astype(BF16)
        else:
            y_s[slot(3, j)] = pair_sum(1, j, low, 1 - y).astype(BF16)
        y_copy(g, j).start()

    def z_copy(i, j):
        at, wide = out_cuts[j]
        spot = (pl.ds(i * rows, rows), pl.ds(at, wide))
        return remote(
            z_s.at[spot], z_r.at[spot], rz_s, rz_r.at[i, j],
            f_dev if i == 1 else n_dev,
        )

    def cross(j):
        y_copy(FAR, j).wait_recv()
        total = pair_sum(0, j, 1 - low, y) + y_r[slot(1, j)].astype(F32)
        z_s[slot(0, j)] = total.astype(BF16)
        z_copy(0, j).start()

    def leap(j):
        z_copy(0, j).wait_recv()
        total = pair_sum(0, j, low, y) + y_r[slot(0, j)].astype(F32)
        total = total + z_r[slot(0, j)].astype(F32)
        z_s[slot(1, j)] = total.astype(BF16)
        z_copy(1, j).start()

    def beside(j):
        y_copy(NEAR, j).wait_recv()
        total = pair_sum(1, j, 1 - low, y) + y_r[slot(2, j)].astype(F32)
        z_s[slot(2, j)] = total.astype(BF16)
        z_copy(2, j).start()

    def finish(j):
        at, wide = out_cuts[j]
        y_copy(OWN, j).wait_recv()
        z_copy(2, j).wait_recv()
        z_copy(1, j).wait_recv()
        total = pair_sum(1, j, low, y) + y_r[slot(3, j)].astype(F32)
        total = total + z_r[slot(2, j)].astype(F32) + z_r[slot(1, j)].astype(F32)
        out_ref[:, at : at + wide] = (
            res_ref[:, at : at + wide].astype(F32) + total
        ).astype(BF16)

    count = len(out_cuts)
    lag = 2
    for n in range(count + lag):
        if n < count:
            product(n)
        if n == count - 1:
            for j in outs:
                core_copy(1, j).start()
        if n >= lag:
            y_send(FAR, n - lag)
    for group in (NEAR, OWN):
        for j in outs:
            y_send(group, j)
    plan = sorted(
        [(j + 0.0, 0, j) for j in outs]
        + [(j + 2.1, 1, j) for j in outs]
        + [(j / 2 + 3.4, 2, j) for j in outs]
    )
    for _, stage, j in plan:
        (cross, leap, beside)[stage](j)
    for j in outs:
        finish(j)
    drain_gather()
    remote(part.at[pl.ds(0, half)], core_r, rc_s, rc_r.at[0, 0], c_dev).wait_send()
    remote(y_s, y_r, ry_s, ry_r.at[0, 0], y_dev).wait_send()
    remote(z_s, z_r, rz_s, rz_r.at[0, 0], n_dev).wait_send()


def fused(residual, norm_gain, expert_ids, expert_weights, gate_proj, up_proj, down_proj):
    rows, model = residual.shape
    hidden = gate_proj.shape[2]
    devices = lax.axis_size("expert")
    experts = devices // 2
    line = devices // 4
    in_cuts = cuts(model, (3, 3, 3, 2))
    ins = len(in_cuts)
    tokens = rows * devices
    width = -(-(model + 2 * experts) // LANES) * LANES
    out_cuts = cuts(model, (2, 3, 3, 3))
    outs = len(out_cuts)
    vmem = pl.BlockSpec(memory_space=pltpu.VMEM)
    hbm = pl.BlockSpec(memory_space=pl.ANY)
    dma = pltpu.SemaphoreType.DMA
    return pl.pallas_call(
        functools.partial(kernel, experts, in_cuts, out_cuts),
        out_shape=pltpu.VMEM((rows, model), BF16),
        in_specs=[vmem] * 4 + [hbm] * 3,
        out_specs=vmem,
        scratch_shapes=[
            pltpu.VMEM((hidden, model), BF16),
            pltpu.VMEM((hidden, model), BF16),
            pltpu.VMEM((hidden, model), BF16),
            pltpu.VMEM((tokens, width), BF16),
            pltpu.VMEM((hidden, tokens), F32),
            pltpu.VMEM((hidden, tokens), F32),
            pltpu.VMEM((tokens, hidden), BF16),
            pltpu.VMEM((tokens, model), BF16),
            pltpu.VMEM((tokens // 2, model), BF16),
            pltpu.VMEM((4 * rows, model), BF16),
            pltpu.VMEM((4 * rows, model), BF16),
            pltpu.VMEM((3 * rows, model), BF16),
            pltpu.VMEM((3 * rows, model), BF16),
            dma((2,)),
            dma,
            dma((ins, line)),
            dma((ins, line)),
            dma((ins, line)),
            dma((ins,)),
            dma((ins, line)),
            dma((ins,)),
            dma((ins,)),
            dma,
            dma((2, outs)),
            dma,
            dma((3, outs)),
            dma,
            dma((3, outs)),
        ],
        compiler_params=pltpu.CompilerParams(
            collective_id=0, has_side_effects=True, vmem_limit_bytes=60 * 1024 * 1024
        ),
    )(
        residual, norm_gain, expert_ids.T, expert_weights.T,
        gate_proj.transpose(0, 2, 1), up_proj.transpose(0, 2, 1), down_proj,
    )


def body(residual, norm_gain, expert_ids, expert_weights, gate_proj, up_proj, down_proj):
    rows = residual.shape[0]
    devices = lax.axis_size("expert")
    capacity = 4 * rows * expert_ids.shape[1] // devices
    dense = capacity >= rows and devices == 16
    form = fused if dense else slotted
    return form(
        residual, norm_gain, expert_ids, expert_weights, gate_proj, up_proj, down_proj
    )


def solution(mesh):
    in_specs = (
        P(("groups", "expert"), None),
        P(),
        P(("groups", "expert"), None),
        P(("groups", "expert"), None),
        P("expert", None, None),
        P("expert", None, None),
        P("expert", None, None),
    )
    out_specs = P(("groups", "expert"), None)
    return jax.shard_map(body, mesh=mesh, in_specs=in_specs, out_specs=out_specs, check_vma=False)
```

time: 40.8 us -> 36.7 us (0.90)
  Pallas kernels: 39.1 us -> 35.9 us
  local copies, waits for them, and re-layouts: 1.54 us -> 0.64 us
    pallas_call x1, Pallas kernels: 39.1 us -> 35.9 us  [fused(): pl.pallas_call(functools.partial(kernel, experts, in_cuts, out_cuts), out...]
    unnamed x1, local copies, waits for them, and re-layouts: 1.54 us -> 0.64 us
where the time goes in v1:
time: 36.7 us; the launch traced here: 36.5 us
  Pallas kernels  35.9 us (98%)
  local copies, waits for them, and re-layouts  0.64 us (2%)
    pallas_call x1, Pallas kernels, fused(): pl.pallas_call(functools.partial(kernel, experts, in_cuts, out_cuts), out...  35.9 us

profile of v1, /device:TPU:0, one launch (start us, length us, event | category | flops | bytes accessed | tf_op | source)
XLA Modules:
  0.0 36.5 jit_solution(9078315123711882442)
XLA Ops:
  0.0 35.9 %shard_map.73 = bf16[16,2880]{1,0:T(8,128)(2,1)S(1)} custom-call(bf16[16,2880]{1,0:T(8,128)(2,1)} %res_ref.1, f32[2880]{0:T(1024)} %gain_ref.1, s32[4,16]{1,0:T(4,128)} %bitcast.6, f32[4,16]{1,0:T(4,128)} %bitcast.7, bf16[1,720,2880]{2,1,0:T(8,128)(2,1)} %bitcast.4, bf16[1,720,2880]{2,1,0:T(8,128)(2,1)} %bitcast.5, bf16[1,720,2880]{2,1,0:T(8,128)(2,1)} %down_hbm.1), custom_call_target="tpu_custom_call" | custom-call | tf_op jit(solution)/shard_map/pallas_call | solution.py:409
  35.9 0.6 %copy.9 = bf16[16,2880]{1,0:T(8,128)(2,1)} copy(bf16[16,2880]{1,0:T(8,128)(2,1)S(1)} %shard_map.73) | data formatting | bytes 184320
